TPU v7x, 32 devices: a whole 2x2x4 slice. The times are simulated.
32 devices in a mesh: dp: 8 (over y, x, core), fsdp: 4 (over z).
Axes of the slice: x: 2, y: 2, z: 4, core: 2. Of those that a mesh axis runs over, the one named last changes fastest.
Arguments:
- tokens: bfloat16 [16384, 1024], P(('dp', 'fsdp')), may hold values from -20 to 20
- w_qkv: bfloat16 [1024, 3072], P('fsdp'), may hold values from -0.1875 to 0.1875
- w_out: bfloat16 [1024, 1024], P('fsdp'), may hold values from -0.1875 to 0.1875
- doc_blocks: int32 [32, 4], P(('dp', 'fsdp')), may hold values from 0 to 1, never falling along the last dimension, each value on 1 to 3 neighbouring positions
- cotangent: bfloat16 [16384, 1024], P(('dp', 'fsdp')), may hold values from -6 to 6
Outputs:
- output: bfloat16 [16384, 1024], P(('dp', 'fsdp'))
- grad_tokens: bfloat16 [16384, 1024], P(('dp', 'fsdp'))
- grad_w_qkv: float32 [1024, 3072], P('fsdp')
- grad_w_out: float32 [1024, 1024], P('fsdp')
Inputs may be any that keep to these rules, and one draw needn't show every extreme that they name: `doc_blocks`: ids never fall along a sequence; each of the 2 documents of a sequence covers 1 to 3 blocks.
All inputs are finite; a program needn't handle non-finite values.
Results may differ from a plain program's by a relative error of at most 0.012.
Values may be sent and summed in bfloat16 or wider, within the bound.
A program may use at most 128 MiB of HBM per device.

v0:
```python
import math
import jax
import jax.numpy as jnp
from jax import lax
from jax.sharding import PartitionSpec as P

H = 8
NEG_FILL = -1e30
CONTRACT_ROWS = (((0,), (0,)), ((), ()))
CONTRACT_COLS = (((1,), (1,)), ((), ()))


def row_mask(doc_ids, row_count):
    block_len = row_count // doc_ids.shape[0]
    doc_rows = jnp.repeat(doc_ids, block_len, total_repeat_length=row_count)
    position = jnp.arange(row_count, dtype=jnp.int32)
    causal = position[None, :] <= position[:, None]
    return causal & (doc_rows[None, :] == doc_rows[:, None])


def split_heads(matrix, head_count):
    return matrix.reshape(matrix.shape[0], head_count, matrix.shape[1] // head_count)


def attend_forward(query_rows, key_rows, value_rows, allowed, head_count):
    row_count = query_rows.shape[0]
    query_heads = split_heads(query_rows, head_count)
    key_heads = split_heads(key_rows, head_count)
    value_heads = split_heads(value_rows, head_count)
    score_scale = query_heads.shape[2] ** (-0.5)
    scores = (
        jnp.einsum("qhd,khd->hqk", query_heads, key_heads, preferred_element_type=jnp.float32)
        * score_scale
    )
    scores = jnp.where(allowed[None], scores, NEG_FILL)
    highest = jnp.max(scores, axis=-1, keepdims=True)
    expvals = jnp.exp(scores - highest)
    attn_probs = expvals / jnp.sum(expvals, axis=-1, keepdims=True)
    probs_half = attn_probs.astype(jnp.bfloat16)
    mixed = jnp.einsum("hqk,khd->qhd", probs_half, value_heads, preferred_element_type=jnp.float32)
    return (mixed.astype(jnp.bfloat16).reshape(row_count, -1), attn_probs, probs_half)


def attend_backward(
    query_rows, key_rows, value_rows, attn_probs, probs_half, grad_mixed, head_count
):
    row_count = query_rows.shape[0]
    query_heads = split_heads(query_rows, head_count)
    key_heads = split_heads(key_rows, head_count)
    value_heads = split_heads(value_rows, head_count)
    grad_heads = split_heads(grad_mixed, head_count)
    score_scale = query_heads.shape[2] ** (-0.5)
    grad_probs = jnp.einsum(
        "qhd,khd->hqk", grad_heads, value_heads, preferred_element_type=jnp.float32
    )
    grad_values = jnp.einsum(
        "hqk,qhd->khd", probs_half, grad_heads, preferred_element_type=jnp.float32
    )
    inner = jnp.sum(attn_probs * grad_probs, axis=-1, keepdims=True)
    grad_scores = (attn_probs * (grad_probs - inner)).astype(jnp.bfloat16)
    grad_queries = (
        jnp.einsum("hqk,khd->qhd", grad_scores, key_heads, preferred_element_type=jnp.float32)
        * score_scale
    )
    grad_keys = (
        jnp.einsum("hqk,qhd->khd", grad_scores, query_heads, preferred_element_type=jnp.float32)
        * score_scale
    )
    pieces_list = [grad_queries, grad_keys, grad_values]
    return jnp.concatenate(
        [p.astype(jnp.bfloat16).reshape(row_count, -1) for p in pieces_list], axis=1
    )


def body(tokens, w_qkv, w_out, doc_blocks, cotangent):
    row_count = tokens.shape[0]
    head_width = w_out.shape[1]
    head_count = H
    all_devices = lax.axis_size("dp") * lax.axis_size("fsdp")
    allowed = row_mask(doc_blocks[0], row_count)
    columns = tokens
    qkv = jnp.dot(
        columns,
        lax.all_gather(w_qkv, "fsdp", axis=0, tiled=True),
        preferred_element_type=jnp.float32,
    ).astype(jnp.bfloat16)
    query_rows = qkv[:, :head_width]
    key_rows = qkv[:, head_width : 2 * head_width]
    value_rows = qkv[:, 2 * head_width :]
    mixed, attn_probs, probs_half = attend_forward(
        query_rows, key_rows, value_rows, allowed, head_count
    )
    output = lax.dot_general(
        mixed,
        lax.all_gather(w_out, "fsdp", axis=0, tiled=True),
        CONTRACT_COLS,
        preferred_element_type=jnp.float32,
    )
    columns = cotangent
    grad_mixed = jnp.dot(
        columns,
        lax.all_gather(w_out, "fsdp", axis=0, tiled=True),
        preferred_element_type=jnp.float32,
    ).astype(jnp.bfloat16)
    output = output.astype(jnp.bfloat16)
    grad_qkv = attend_backward(
        query_rows, key_rows, value_rows, attn_probs, probs_half, grad_mixed, head_count
    )
    grad_tokens = lax.dot_general(
        grad_qkv,
        lax.all_gather(w_qkv, "fsdp", axis=0, tiled=True),
        CONTRACT_COLS,
        preferred_element_type=jnp.float32,
    )
    grad_tokens = grad_tokens.astype(jnp.bfloat16)
    first_term = lax.dot_general(
        tokens, grad_qkv, CONTRACT_ROWS, preferred_element_type=jnp.float32
    )
    second_term = lax.dot_general(
        cotangent, mixed, CONTRACT_ROWS, preferred_element_type=jnp.float32
    )
    partial_grad = lax.psum_scatter(
        jnp.concatenate([first_term, second_term], axis=1), "fsdp", scatter_dimension=0, tiled=True
    )
    summed = lax.psum(partial_grad, "dp")
    norm_factor = 1.0 / math.sqrt(row_count * all_devices)
    grad_w_qkv = summed[:, : 3 * head_width] * norm_factor
    grad_w_out = summed[:, 3 * head_width :] * norm_factor
    return (output, grad_tokens, grad_w_qkv, grad_w_out)


def solution(mesh):
    placed = (
        P(("dp", "fsdp"), None),
        P("fsdp", None),
        P("fsdp", None),
        P(("dp", "fsdp"), None),
        P(("dp", "fsdp"), None),
    )
    return jax.shard_map(
        body,
        mesh=mesh,
        in_specs=placed,
        out_specs=(
            P(("dp", "fsdp"), None),
            P(("dp", "fsdp"), None),
            P("fsdp", None),
            P("fsdp", None),
        ),
        check_vma=False,
    )
```

profile of v0, /device:TPU:0, one launch (start us, length us, event | category | flops | bytes accessed | tf_op | source)
XLA Modules:
  0.0 596.9 jit_solution(12965069515736910643)
XLA Ops:
  7.2 0.0 copy-start
  7.2 0.0 all-gather.5.cloned.1.call-start
  7.2 0.7 all-gather.5.cloned.1.call-update
  7.9 0.0 all-gather.3.cloned.1.call-start
  8.0 0.7 all-gather.3.cloned.1.call-update
  8.7 0.0 reduce-scatter.2.cloned.1.call-start
  8.7 1.4 fusion.30
  10.1 2.6 compare_select_fusion.1
  12.7 0.2 fusion.18
  13.0 45.0 %all-gather.5.cloned.1.call-done = bf16[1024,1024]{1,0:T(8,128)(2,1)} async-done(((bf16[256,1024]{1,0:T(8,128)(2,1)}), bf16[1024,1024]{1,0:T(8,128)(2,1)}) %all-gather.5.cloned.1.call-update) | async-done | bytes 2097168 | tf_op jit(solution)/shard_map/all_gather | solution.py:95
  58.0 3.2 convolution_convert_fusion.1
  61.1 1.3 copy.29
  62.5 111.2 %all-gather.3.cloned.1.call-done = bf16[1024,3072]{1,0:T(8,128)(2,1)} async-done(((bf16[256,3072]{1,0:T(8,128)(2,1)}), bf16[1024,3072]{1,0:T(8,128)(2,1)}) %all-gather.3.cloned.1.call-update) | async-done | bytes 6291472 | tf_op jit(solution)/shard_map/all_gather | solution.py:84
  173.7 0.0 copy-done
  173.7 6.4 %convolution_convert_fusion = bf16[512,3072]{1,0:T(8,128)(2,1)S(1)} fusion(bf16[512,1024]{1,0:T(8,128)(2,1)S(1)} %copy-done, bf16[1024,3072]{1,0:T(8,128)(2,1)} %all-gather.3.cloned.1.call-done), kind=kOutput, calls=%fused_computation.8 | convolution fusion | flops 3222798336 | bytes 10485760 | tf_op jit(solution)/shard_map/dot_general | solution.py:82
  180.1 1.8 fusion.29
  181.9 0.5 copy.27
  182.5 1.5 copy.28
  184.0 5.4 fusion.31
  189.4 0.0 copy-start.1
  189.4 0.0 copy-start.2
  189.4 4.7 fusion.9
  194.1 0.0 copy-start.9
  194.2 1.7 copy-done.1
  195.9 0.2 copy-done.2
  196.1 0.0 copy-start.5
  196.1 1.5 fusion.12
  197.6 0.0 copy-done.5
  197.6 0.0 copy-start.7
  197.7 1.5 multiply_reduce_fusion
  199.2 2.7 multiply_convert_fusion
  201.9 1.5 multiply_convert_fusion.1
  203.4 0.0 copy-start.3
  203.4 0.0 copy-start.6
  203.4 0.7 multiply_convert_fusion.2
  204.1 0.0 copy-done.9
  204.1 0.9 copy-done.6
  205.0 1.3 convolution_bitcast_fusion.1
  206.3 0.0 copy-done.7
  206.3 0.0 copy-done.3
  206.3 3.5 convolution_bitcast_fusion
  209.8 7.2 %pad_maximum_fusion = f32[1024,4096]{0,1:T(8,128)} fusion(f32[1024,1024]{0,1:T(8,128)S(1)} %convolution_bitcast_fusion.1, f32[1024,3072]{0,1:T(8,128)S(1)} %convolution_bitcast_fusion), kind=kLoop, calls=%fused_computation.1 | loop fusion | flops 4194304 | bytes 33554432 | tf_op jit(solution)/shard_map/concatenate | solution.py:123
  217.1 0.0 reduce-scatter.2.cloned.1.call-update
  217.1 0.0 copy-start.10
  217.1 0.0 all-reduce.2.cloned.1.call-start
  217.2 278.7 %reduce-scatter.2.cloned.1.call-done = f32[256,4096]{0,1:T(8,128)} async-done(((f32[1024,4096]{0,1:T(8,128)}), f32[256,4096]{0,1:T(8,128)}) %reduce-scatter.2.cloned.1.call-update) | async-done | bytes 4194320 | tf_op jit(solution)/shard_map/reduce_scatter | solution.py:122
  495.8 0.0 all-reduce.2.cloned.1.call-update
  495.9 0.0 copy-done.10
  495.9 0.0 copy-start.4
  495.9 0.0 copy-start.8
  495.9 4.0 convolution_convert_fusion.2
  499.9 0.0 copy-done.4
  499.9 0.0 copy-done.8
  499.9 7.2 %convolution_convert_fusion.3 = bf16[512,1024]{1,0:T(8,128)(2,1)} fusion(bf16[1024,3072]{1,0:T(8,128)(2,1)} %all-gather.3.cloned.1.call-done, bf16[512,1024]{0,1:T(8,128)(2,1)S(1)} %bitcast.77, bf16[512,1024]{0,1:T(8,128)(2,1)S(1)} %bitcast.70, bf16[512,1024]{0,1:T(8,128)(2,1)S(1)} %bitcast.72), kind=kOutput, calls=%fused_computation.26 | convolution fusion | flops 3231186944 | bytes 10485760 | tf_op jit(solution)/shard_map/dot_general | solution.py:109
  507.1 73.3 %all-reduce.2.cloned.1.call-done = f32[256,4096]{0,1:T(8,128)} async-done(((f32[256,4096]{0,1:T(8,128)}), f32[256,4096]{0,1:T(8,128)}) %all-reduce.2.cloned.1.call-update) | async-done | bytes 4194320 | tf_op jit(solution)/shard_map/psum | solution.py:125
  580.4 3.8 slice_multiply_fusion
  584.2 3.5 copy.21
  587.8 1.3 slice_multiply_fusion.1
  589.1 1.3 copy.22
  (3 shorter events, 0.0 us)
Async XLA Ops:
  7.2 166.5 %copy-start = (bf16[512,1024]{1,0:T(8,128)(2,1)S(1)}, bf16[512,1024]{1,0:T(8,128)(2,1)}, u32[]{:S(2)}) copy-start(bf16[512,1024]{1,0:T(8,128)(2,1)} %param.7) | copy-start | bytes 3145732
  7.2 50.8 %all-gather.5.cloned.1.call-start = ((), (), s32[]{:S(2)}) async-start(), calls=%async_computation.2 | async-start | bytes 2621440 | tf_op jit(solution)/shard_map/all_gather | solution.py:95
  7.9 165.8 %all-gather.3.cloned.1.call-start = ((), (), s32[]{:S(2)}) async-start(), calls=%async_computation.1 | async-start | bytes 7864320 | tf_op jit(solution)/shard_map/all_gather | solution.py:84
  8.7 487.2 %reduce-scatter.2.cloned.1.call-start = ((), (), s32[]{:S(2)}) async-start(), calls=%async_computation.3 | async-start | bytes 20971520 | tf_op jit(solution)/shard_map/reduce_scatter | solution.py:122
  189.4 6.5 %copy-start.1 = (f32[8,512,512]{1,2,0:T(8,128)S(1)}, f32[8,512,512]{1,2,0:T(8,128)}, u32[]{:S(2)}) copy-start(f32[8,512,512]{1,2,0:T(8,128)} %get-tuple-element.28) | copy-start | bytes 25165828
  189.4 6.7 %copy-start.2 = (bf16[512,1024]{0,1:T(8,128)(2,1)S(1)}, bf16[512,1024]{0,1:T(8,128)(2,1)}, u32[]{:S(2)}) copy-start(bf16[512,1024]{0,1:T(8,128)(2,1)} %copy.29) | copy-start | bytes 3145732
  194.1 10.0 %copy-start.9 = (bf16[8,128,512]{2,1,0:T(8,128)(2,1)}, bf16[8,128,512]{2,1,0:T(8,128)(2,1)S(1)}, u32[]{:S(2)}) copy-start(bf16[8,128,512]{2,1,0:T(8,128)(2,1)S(1)} %fusion.9) | copy-start | bytes 3145732
  196.1 1.5 copy-start.5
  197.6 8.6 %copy-start.7 = (bf16[8,128,512]{2,1,0:T(8,128)(2,1)}, bf16[8,128,512]{2,1,0:T(8,128)(2,1)S(1)}, u32[]{:S(2)}) copy-start(bf16[8,128,512]{2,1,0:T(8,128)(2,1)S(1)} %fusion.12) | copy-start | bytes 3145732
  203.4 2.9 copy-start.3
  203.4 1.6 copy-start.6
  217.1 278.8 %copy-start.10 = (bf16[8,128,512]{2,1,0:T(8,128)(2,1)S(1)}, bf16[8,128,512]{2,1,0:T(8,128)(2,1)}, u32[]{:S(2)}) copy-start(bf16[8,128,512]{2,1,0:T(8,128)(2,1)} %copy-done.9) | copy-start | bytes 3145732
  217.1 363.3 %all-reduce.2.cloned.1.call-start = ((), (), s32[]{:S(2)}) async-start(), calls=%async_computation.4 | async-start | bytes 8388608 | tf_op jit(solution)/shard_map/psum | solution.py:125
  495.9 4.0 copy-start.4
  495.9 4.0 copy-start.8
Sparse Core Ops, SparseCore 0:
  9.6 48.3 all-gather.4
  59.5 114.1 all-gather.2
  217.2 278.5 reduce-scatter.1
  499.0 81.4 all-reduce.1
where the time goes:
time: 597 us
  waiting for transfers between devices  510 us (85%)
  matrix products  41 us (7%)
  other arithmetic  17.8 us (3%)
  local copies, waits for them, and re-layouts  14.3 us (2%)
  between operations  14 us (2%)
    reduce_scatter x1, waiting for transfers between devices, body(): lax.psum_scatter(jnp.concatenate([first_term, second_term], axis=1), 'fsd...  279 us
    all_gather x1, waiting for transfers between devices, body(): lax.all_gather(w_qkv, 'fsdp', axis=0, tiled=True)  111 us
    psum x1, waiting for transfers between devices, body(): summed = lax.psum(partial_grad, 'dp')  73.3 us
    all_gather x1, waiting for transfers between devices, body(): lax.all_gather(w_out, 'fsdp', axis=0, tiled=True)  45 us
  transfers between devices with their start and end apart: 4, of which 4 were waited for; matrix products, arithmetic and copies ran while one was open for 3% of the time, Pallas kernels for 0%

commit v1 on v0

--- a/solution.py
+++ b/solution.py
@@ -3,6 +3,7 @@
 import jax.numpy as jnp
 from jax import lax
 from jax.sharding import PartitionSpec as P
+from jax.lax import all_gather
 
 H = 8
 NEG_FILL = -1e30
@@ -122,7 +123,8 @@
     partial_grad = lax.psum_scatter(
         jnp.concatenate([first_term, second_term], axis=1), "fsdp", scatter_dimension=0, tiled=True
     )
-    summed = lax.psum(partial_grad, "dp")
+    step_out = all_gather(partial_grad, "dp")
+    summed = jnp.sum(step_out, axis=0)
     norm_factor = 1.0 / math.sqrt(row_count * all_devices)
     grad_w_qkv = summed[:, : 3 * head_width] * norm_factor
     grad_w_out = summed[:, 3 * head_width :] * norm_factor

time: 597 us -> 723 us (1.21)
  waiting for transfers between devices: 510 us -> 595 us
  other arithmetic: 17.8 us -> 39.5 us
  local copies, waits for them, and re-layouts: 14.3 us -> 32.6 us
    all_gather x0 -> x1, waiting for transfers between devices: none -> 158 us  [body(): step_out = all_gather(partial_grad, 'dp')]
    psum x1 -> x0, waiting for transfers between devices: 73.3 us -> none  [body(): summed = lax.psum(partial_grad, 'dp')]
    reduce_sum x0 -> x1, other arithmetic: none -> 21.7 us  [body(): summed = jnp.sum(step_out, axis=0)]
    unnamed x24 -> x25, local copies, waits for them, and re-layouts: 7.69 us -> 26 us
where the time goes in v1:
time: 723 us; the launch traced here: 722 us
  waiting for transfers between devices  595 us (82%)
  matrix products  41.3 us (6%)
  other arithmetic  39.5 us (5%)
  local copies, waits for them, and re-layouts  32.6 us (5%)
  between operations  14 us (2%)
    reduce_scatter x1, waiting for transfers between devices, body(): lax.psum_scatter(jnp.concatenate([first_term, second_term], axis=1), 'fsd...  279 us
    all_gather x1, waiting for transfers between devices, body(): step_out = all_gather(partial_grad, 'dp')  158 us
    all_gather x1, waiting for transfers between devices, body(): lax.all_gather(w_qkv, 'fsdp', axis=0, tiled=True)  111 us
    all_gather x1, waiting for transfers between devices, body(): lax.all_gather(w_out, 'fsdp', axis=0, tiled=True)  45 us
    unnamed x25, local copies, waits for them, and re-layouts  26 us
    reduce_sum x1, other arithmetic, body(): summed = jnp.sum(step_out, axis=0)  21.7 us
  transfers between devices with their start and end apart: 4, of which 4 were waited for; matrix products, arithmetic and copies ran while one was open for 3% of the time, Pallas kernels for 0%

profile of v1, /device:TPU:0, one launch (start us, length us, event | category | flops | bytes accessed | tf_op | source)
XLA Modules:
  0.0 722.1 jit_solution(15414473233562654689)
XLA Ops:
  7.2 0.0 copy-start
  7.2 0.0 all-gather.7.cloned.1.call-start
  7.2 0.7 all-gather.7.cloned.1.call-update
  7.9 0.0 all-gather.5.cloned.1.call-start
  8.0 0.7 all-gather.5.cloned.1.call-update
  8.7 0.0 reduce-scatter.2.cloned.1.call-start
  8.7 1.4 fusion.30
  10.1 2.6 compare_select_fusion.1
  12.7 0.2 fusion.18
  13.0 45.0 %all-gather.7.cloned.1.call-done = bf16[1024,1024]{1,0:T(8,128)(2,1)} async-done(((bf16[256,1024]{1,0:T(8,128)(2,1)}), bf16[1024,1024]{1,0:T(8,128)(2,1)}) %all-gather.7.cloned.1.call-update) | async-done | bytes 2097168 | tf_op jit(solution)/shard_map/all_gather | solution.py:96
  58.0 3.2 convolution_convert_fusion.1
  61.1 1.3 copy.41
  62.5 111.2 %all-gather.5.cloned.1.call-done = bf16[1024,3072]{1,0:T(8,128)(2,1)} async-done(((bf16[256,3072]{1,0:T(8,128)(2,1)}), bf16[1024,3072]{1,0:T(8,128)(2,1)}) %all-gather.5.cloned.1.call-update) | async-done | bytes 6291472 | tf_op jit(solution)/shard_map/all_gather | solution.py:85
  173.7 0.0 copy-done
  173.7 6.4 convolution_convert_fusion
  180.1 1.8 fusion.29
  181.9 0.5 copy.40
  182.4 1.5 copy.39
  183.9 5.4 fusion.31
  189.4 0.0 copy-start.2
  189.4 0.0 copy-start.6
  189.4 5.3 fusion.12
  194.7 0.0 copy-start.8
  194.7 0.7 copy-done.2
  195.4 0.3 copy-done.6
  195.7 0.0 copy-start.3
  195.7 1.0 fusion.9
  196.7 0.3 copy-done.3
  196.9 0.0 copy-start.10
  196.9 1.5 multiply_reduce_fusion
  198.4 2.7 multiply_convert_fusion
  201.1 0.0 copy-start.7
  201.1 1.5 multiply_convert_fusion.1
  202.6 0.0 copy-start.4
  202.6 0.7 multiply_convert_fusion.2
  203.3 0.0 copy-done.10
  203.3 0.0 copy-done.7
  203.4 1.3 convolution_bitcast_fusion.1
  204.6 0.0 copy-done.8
  204.6 0.0 copy-done.4
  204.6 3.6 convolution_bitcast_fusion
  208.2 7.1 pad_maximum_fusion
  215.3 0.0 reduce-scatter.2.cloned.1.call-update
  215.3 0.0 all-gather.9.cloned.1.call-start
  215.4 278.8 %reduce-scatter.2.cloned.1.call-done = f32[256,4096]{0,1:T(8,128)} async-done(((f32[1024,4096]{0,1:T(8,128)}), f32[256,4096]{0,1:T(8,128)}) %reduce-scatter.2.cloned.1.call-update) | async-done | bytes 4194320 | tf_op jit(solution)/shard_map/reduce_scatter | solution.py:123
  494.2 0.0 copy-start.5
  494.2 0.0 copy-start.9
  494.2 0.0 all-gather.9.cloned.1.call-update
  494.2 4.3 convolution_convert_fusion.2
  498.5 0.0 copy-done.5
  498.5 0.0 copy-done.9
  498.5 7.2 convolution_convert_fusion.3
  505.7 158.1 %all-gather.9.cloned.1.call-done = f32[2048,4096]{0,1:T(8,128)} async-done(((f32[256,4096]{0,1:T(8,128)}), f32[2048,4096]{0,1:T(8,128)}) %all-gather.9.cloned.1.call-update) | async-done | bytes 33554448 | tf_op jit(solution)/shard_map/all_gather | solution.py:126
  663.9 19.9 %copy.43 = f32[512,8,8,256]{3,2,1,0:T(8,128)S(1)} copy(f32[512,8,8,256]{3,1,2,0:T(8,128)} %bitcast.68) | data formatting | bytes 67108864
  683.8 21.7 %bitcast_reduce_fusion = f32[256,4096]{0,1:T(8,128)} fusion(f32[512,8,8,256]{3,2,1,0:T(8,128)S(1)} %copy.43), kind=kLoop, calls=%fused_computation.1 | loop fusion | flops 7340032 | bytes 37748736 | tf_op jit(solution)/shard_map/reduce_sum | solution.py:127
  705.5 0.0 copy-start.1
  705.5 1.4 slice_multiply_fusion.1
  706.9 3.8 slice_multiply_fusion
  710.7 3.5 copy.33
  714.2 1.3 copy.34
  715.5 0.0 copy-done.1
  (3 shorter events, 0.0 us)
Async XLA Ops:
  7.2 166.5 %copy-start = (bf16[512,1024]{1,0:T(8,128)(2,1)S(1)}, bf16[512,1024]{1,0:T(8,128)(2,1)}, u32[]{:S(2)}) copy-start(bf16[512,1024]{1,0:T(8,128)(2,1)} %param.7) | copy-start | bytes 3145732
  7.2 50.8 %all-gather.7.cloned.1.call-start = ((), (), s32[]{:S(2)}) async-start(), calls=%async_computation.2 | async-start | bytes 2621440 | tf_op jit(solution)/shard_map/all_gather | solution.py:96
  7.9 165.8 %all-gather.5.cloned.1.call-start = ((), (), s32[]{:S(2)}) async-start(), calls=%async_computation.1 | async-start | bytes 7864320 | tf_op jit(solution)/shard_map/all_gather | solution.py:85
  8.7 485.5 %reduce-scatter.2.cloned.1.call-start = ((), (), s32[]{:S(2)}) async-start(), calls=%async_computation.3 | async-start | bytes 20971520 | tf_op jit(solution)/shard_map/reduce_scatter | solution.py:123
  189.4 6.1 copy-start.2
  189.4 6.3 copy-start.6
  194.7 9.9 %copy-start.8 = (bf16[8,128,512]{2,1,0:T(8,128)(2,1)}, bf16[8,128,512]{2,1,0:T(8,128)(2,1)S(1)}, u32[]{:S(2)}) copy-start(bf16[8,128,512]{2,1,0:T(8,128)(2,1)S(1)} %fusion.12) | copy-start | bytes 3145732
  195.7 1.2 copy-start.3
  196.9 6.4 copy-start.10
  201.1 2.3 copy-start.7
  202.6 2.0 copy-start.4
  215.3 448.5 %all-gather.9.cloned.1.call-start = ((), (), s32[]{:S(2)}) async-start(), calls=%async_computation.4 | async-start | bytes 37748736 | tf_op jit(solution)/shard_map/all_gather | solution.py:126
  494.2 4.4 copy-start.5
  494.2 4.4 copy-start.9
  705.5 10.0 %copy-start.1 = (bf16[512,1024]{1,0:T(8,128)(2,1)S(1)}, bf16[512,1024]{1,0:T(8,128)(2,1)}, u32[]{:S(2)}) copy-start(bf16[512,1024]{1,0:T(8,128)(2,1)} %param.7) | copy-start | bytes 3145732
Sparse Core Ops, SparseCore 0:
  9.6 48.3 all-gather.6
  59.5 114.1 all-gather.4
  215.5 278.6 reduce-scatter.1
  495.9 167.9 all-gather.8
